TPU v7x, 256 devices: a whole 4x4x8 slice. The times are simulated.
256 devices in a mesh: slab: 64 (over y, x, z_hi), pt: 4 (over z_lo, core).
Axes of the slice: x: 4, y: 4, z: 8 (z_hi: 4, z_lo: 2; z = z_hi * 2 + z_lo), core: 2. Of those that a mesh axis runs over, the one named last changes fastest.
Arguments:
- orbitals: bfloat16 [131072, 256], P('slab'), may hold values from -6 to 6
- potential: float32 [131072], P('slab'), may hold values from -1 to 1
- fit_matrix: bfloat16 [131072, 8192], P('slab', 'pt'), may hold values from -0.00390625 to 0.00390625
- owner_rows: int32 [4, 64, 64], P(None, 'slab'), may hold values from 0 to 2047, as said below
- owner_count: int32 [4, 64], replicated, may hold values from 0 to 64, as said below
Outputs:
- filtered: bfloat16 [131072, 256], P('slab')
Inputs may be any that keep to these rules, and one draw needn't show every extreme that they name: `owner_count`: for each block p the counts over slabs sum to 2048, and in every block some slab lists exactly 64 points. `owner_rows`: the listed entries (c < owner_count[p, s]) of slab s are distinct over all blocks p and slots c; the other entries are 0.
All inputs are finite; a program needn't handle non-finite values.
Results may differ from a plain program's by a relative error of at most 0.0054.
Values may be sent and summed in bfloat16 or wider, within the bound.
No kernel may reach another device: no remote copies, remote signals or barrier semaphores. Data moves between devices by JAX's collectives and lax.ppermute only.
A program may use at most 64 MiB of HBM per device.

v0:
```python
import jax
import jax.numpy as jnp
from jax import lax
from jax.sharding import PartitionSpec as P

DEG = 2
CZ = 8
NY = 8
NX = 32
stencil_coef = (-205.0 / 72.0, 8.0 / 5.0, -1.0 / 5.0, 8.0 / 315.0, -1.0 / 560.0)


def extended(cells, sides, width):
    for axis, dim in sides:
        count = lax.axis_size(axis)
        head = lax.slice_in_dim(cells, 0, width, axis=dim)
        tail = lax.slice_in_dim(cells, cells.shape[dim] - width, cells.shape[dim], axis=dim)
        cells = jnp.concatenate(
            [
                lax.ppermute(tail, axis, [(i, (i + 1) % count) for i in range(count)]),
                cells,
                lax.ppermute(head, axis, [((i + 1) % count, i) for i in range(count)]),
            ],
            axis=dim,
        )
    return cells


def plane_table():
    cell_ids = jnp.arange(NY * NX, dtype=jnp.int32)
    row_y = cell_ids // NX
    col_x = cell_ids % NX
    diff_y = (row_y[:, None] - row_y[None, :]) % NY
    diff_x = (col_x[:, None] - col_x[None, :]) % NX
    same_y = row_y[:, None] == row_y[None, :]
    same_x = col_x[:, None] == col_x[None, :]
    table = jnp.zeros((NY * NX, NY * NX), jnp.float32)
    for offset in range(1, 5):
        along_x = (same_y & (diff_x == offset % NX)).astype(jnp.float32) + (
            same_y & (diff_x == -offset % NX)
        ).astype(jnp.float32)
        along_y = (same_x & (diff_y == offset % NY)).astype(jnp.float32) + (
            same_x & (diff_y == -offset % NY)
        ).astype(jnp.float32)
        table = table + stencil_coef[offset] * (along_x + along_y)
    return table


def local_terms(vectors, potential):
    share_cols = vectors.shape[1]
    blocked = vectors.reshape(CZ, NY * NX, share_cols)
    padded = extended(blocked, (("slab", 0),), 4)
    center = blocked.astype(jnp.float32)
    in_plane = jnp.einsum(
        "pq,zqb->zpb",
        plane_table(),
        center,
        precision=lax.Precision.HIGHEST,
        preferred_element_type=jnp.float32,
    )
    summed = 3.0 * stencil_coef[0] * center + in_plane
    for offset in range(1, 5):
        upper = padded[4 + offset : 4 + offset + CZ].astype(jnp.float32)
        lower = padded[4 - offset : 4 - offset + CZ].astype(jnp.float32)
        summed = summed + stencil_coef[offset] * (upper + lower)
    kinetic = (-0.5 * summed).reshape(CZ * NY * NX, share_cols)
    return kinetic + potential[:, None] * center.reshape(CZ * NY * NX, share_cols)


def point_positions(count_row, capacity, point_total):
    inclusive = jnp.cumsum(count_row)
    point_ranks = jnp.arange(point_total, dtype=jnp.int32)
    before = (inclusive[None, :] <= point_ranks[:, None]).astype(jnp.int32)
    slab_of = jnp.sum(before, axis=1)
    base_count = jnp.sum(before * count_row[None, :], axis=1)
    return slab_of * capacity + point_ranks - base_count


def chebyshev(column_part, first_points, apply_op, next_points):
    previous = column_part
    current = column_part
    field_points = first_points
    for turn_number in range(DEG):
        applied = apply_op(current, field_points)
        scaled = applied - 3.5 * current.astype(jnp.float32)
        if turn_number == 0:
            upcoming = (scaled / 4.0).astype(jnp.bfloat16)
        else:
            upcoming = (0.5 * scaled - previous.astype(jnp.float32)).astype(jnp.bfloat16)
        previous, current = (current, upcoming)
        if turn_number + 1 < DEG:
            field_points = next_points(current)
    return current


def body(orbitals, potential, fit_matrix, owner_rows, owner_count):
    block_index = lax.axis_index("pt")
    capacity = owner_rows.shape[2]
    all_rows = owner_rows[:, 0, :]
    mine_rows = lax.dynamic_index_in_dim(all_rows, block_index, 0, keepdims=False)
    count_row = lax.dynamic_index_in_dim(owner_count, block_index, 0, keepdims=False)
    positions = point_positions(count_row, capacity, fit_matrix.shape[1])

    def gather_points(vectors):
        picked = jnp.take(vectors, mine_rows, axis=0)
        gathered = lax.all_gather(picked, "slab", axis=0, tiled=True)
        return jnp.take(gathered, positions, axis=0)

    psi_points = gather_points(orbitals)
    density = lax.dot_general(
        orbitals, psi_points, (((1,), (1,)), ((), ())), preferred_element_type=jnp.float32
    )
    kernel = (fit_matrix.astype(jnp.float32) * density).astype(jnp.bfloat16)

    def apply_whole(vectors, field_points):
        partial_value = jnp.dot(kernel, field_points, preferred_element_type=jnp.float32)
        exch_term = lax.psum(partial_value, "pt")
        return local_terms(vectors, potential) - exch_term

    return chebyshev(orbitals, psi_points, apply_whole, gather_points)


def solution(mesh):
    placed = (P("slab", None), P("slab"), P("slab", "pt"), P(None, "slab", None), P())
    return jax.shard_map(
        body, mesh=mesh, in_specs=placed, out_specs=P("slab", None), check_vma=False
    )
```

profile of v0, /device:TPU:1, one launch (start us, length us, event | category | flops | bytes accessed | tf_op | source)
XLA Modules:
  0.0 368.9 jit_solution(4444609752312211204)
XLA Ops:
  6.5 0.7 compare_and_fusion.16
  7.2 2.0 gather_fusion
  9.2 0.7 broadcast_select_fusion.4
  10.0 12.3 %copy.10 = bf16[2048,2048]{0,1:T(8,128)(2,1)} copy(bf16[2048,2048]{1,0:T(8,128)(2,1)} %param.11) | data formatting | bytes 16777216 | tf_op args[2]
  22.3 0.7 fusion.52
  23.1 0.1 reduce
  23.3 0.2 convert_reduce_fusion
  23.5 67.2 %all-gather.3.cloned.1.call-done = bf16[4096,256]{1,0:T(8,128)(2,1)} async-done(((bf16[64,256]{1,0:T(8,128)(2,1)}), bf16[4096,256]{1,0:T(8,128)(2,1)}) %all-gather.3.cloned.1.call-update) | async-done | bytes 2097168 | tf_op jit(solution)/shard_map/all_gather | solution.py:106
  90.7 8.5 %gather_fusion.1 = bf16[2048,256]{1,0:T(8,128)(2,1)S(1)} fusion(bf16[4096,256]{1,0:T(8,128)(2,1)} %all-gather.3.cloned.1.call-done, s32[2048]{0:T(1024)S(1)} %broadcast_clamp_fusion), kind=kCustom, calls=%fused_computation.1.clone | custom fusion | bytes 2105344 | tf_op jit(solution)/shard_map/jit(_take)/gather | solution.py:107
  99.3 4.8 %fusion = bf16[2048,2048]{0,1:T(8,128)(2,1)S(1)} fusion(bf16[2048,2048]{0,1:T(8,128)(2,1)} %copy.10, bf16[2048,256]{1,0:T(8,128)(2,1)S(1)} %copy-done.1, bf16[2048,256]{1,0:T(8,128)(2,1)S(1)} %gather_fusion.1, pred[2048]{0:T(1024)(128)(4,1)S(1)} %compare_and_fusion.15), kind=kOutput, calls=%fused_computation.5 | convolution fusion | flops 2160590848 | bytes 18876416 | tf_op jit(solution)/shard_map/dot_general | solution.py:110
  104.1 3.2 copy-done
  107.3 4.2 %fusion.37 = f32[2048,256]{1,0:T(8,128)} fusion(bf16[2048,2048]{0,1:T(8,128)(2,1)S(1)} %fusion, bf16[2048,256]{1,0:T(8,128)(2,1)S(1)} %gather_fusion.1, pred[2048]{0:T(1024)(128)(4,1)S(1)} %compare_and_fusion.15), kind=kOutput, calls=%fused_computation.102 | convolution fusion | flops 2148007936 | bytes 11536384 | tf_op jit(solution)/shard_map/dot_general | solution.py:116
  111.7 2.5 collective-permute-start.1
  114.3 5.3 %collective-permute-start = (bf16[4,256,256]{2,1,0:T(8,128)(2,1)S(1)}, bf16[4,256,256]{2,1,0:T(8,128)(2,1)S(1)}, u32[]{:S(2)}, u32[]{:S(2)}) collective-permute-start(bf16[4,256,256]{2,1,0:T(8,128)(2,1)S(1)} %bitcast.61), channel_id=1, source_target_pairs={{4,0},{8,4},{12,8},{16,12},{20,16},{24,20},{28,24},{32,28},{36,32}... | collective-permute-start | bytes 1572872 | tf_op jit(solution)/shard_map/ppermute | solution.py:22
  119.6 9.3 %collective-permute-done.1 = bf16[4,256,256]{2,1,0:T(8,128)(2,1)S(1)} collective-permute-done((bf16[4,256,256]{2,1,0:T(8,128)(2,1)S(1)}, bf16[4,256,256]{2,1,0:T(8,128)(2,1)S(1)}, u32[]{:S(2)}, u32[]{:S(2)}) %collective-permute-start.1) | collective-permute-done | bytes 524320 | tf_op jit(solution)/shard_map/ppermute | solution.py:20
  128.9 5.9 %collective-permute-done = bf16[4,256,256]{2,1,0:T(8,128)(2,1)S(1)} collective-permute-done((bf16[4,256,256]{2,1,0:T(8,128)(2,1)S(1)}, bf16[4,256,256]{2,1,0:T(8,128)(2,1)S(1)}, u32[]{:S(2)}, u32[]{:S(2)}) %collective-permute-start) | collective-permute-done | bytes 524320 | tf_op jit(solution)/shard_map/ppermute | solution.py:22
  134.8 5.7 %fusion.20 = f32[8,256,256]{2,1,0:T(8,128)} fusion(bf16[8,256,256]{2,1,0:T(8,128)(2,1)S(1)} %bitcast.59, bf16[4,256,256]{2,1,0:T(8,128)(2,1)S(1)} %collective-permute-done.1, bf16[4,256,256]{2,1,0:T(8,128)(2,1)S(1)} %collective-permute-done, s32[256]{0:T(256)S(1)} %get-tuple-element.17, s32[256]{0:T(256)S(1)} %get-tuple-element.18), kind=kOutput, calls=%fused_computation.44 | convolution fusion | flops 1633288192 | bytes 5246976 | tf_op jit(solution)/shard_map/pq,zqb->zpb/dot_general | solution.py:54
  140.5 46.3 %all-reduce.3.cloned.1.call-done = f32[2048,256]{1,0:T(8,128)} async-done(((f32[2048,256]{1,0:T(8,128)}), f32[2048,256]{1,0:T(8,128)}) %all-reduce.3.cloned.1.call-update) | async-done | bytes 2097168 | tf_op jit(solution)/shard_map/psum | solution.py:117
  186.8 2.8 fusion.9
  189.6 0.7 gather_fusion.2
  190.3 0.7 broadcast_select_fusion.3
  191.0 0.2 all-reduce.5.cloned.1.call-start
  191.2 76.1 %all-gather.5.cloned.1.call-done = bf16[4096,256]{1,0:T(8,128)(2,1)} async-done(((bf16[64,256]{1,0:T(8,128)(2,1)}), bf16[4096,256]{1,0:T(8,128)(2,1)}) %all-gather.5.cloned.1.call-update) | async-done | bytes 2097168 | tf_op jit(solution)/shard_map/all_gather | solution.py:106
  267.3 8.5 %gather_fusion.3 = bf16[2048,256]{1,0:T(8,128)(2,1)S(1)} fusion(bf16[4096,256]{1,0:T(8,128)(2,1)} %all-gather.5.cloned.1.call-done, s32[2048]{0:T(1024)S(1)} %broadcast_clamp_fusion), kind=kCustom, calls=%fused_computation.3.clone | custom fusion | bytes 2105344 | tf_op jit(solution)/shard_map/jit(_take)/gather | solution.py:107
  275.8 7.5 %fusion.33 = f32[2048,256]{1,0:T(8,128)} fusion(bf16[2048,2048]{0,1:T(8,128)(2,1)} %copy-done, bf16[2048,256]{1,0:T(8,128)(2,1)S(1)} %gather_fusion.3, pred[2048]{0:T(1024)(128)(4,1)S(1)} %compare_and_fusion.15), kind=kOutput, calls=%fused_computation.73 | convolution fusion | flops 2148007936 | bytes 11536384 | tf_op jit(solution)/shard_map/dot_general | solution.py:116
  283.4 2.5 collective-permute-start.3
  285.9 5.3 %collective-permute-start.2 = (bf16[4,256,256]{2,1,0:T(8,128)(2,1)S(1)}, bf16[4,256,256]{2,1,0:T(8,128)(2,1)S(1)}, u32[]{:S(2)}, u32[]{:S(2)}) collective-permute-start(bf16[4,256,256]{2,1,0:T(8,128)(2,1)S(1)} %bitcast.63), channel_id=1, source_target_pairs={{4,0},{8,4},{12,8},{16,12},{20,16},{24,20},{28,24},{32,28},{36,32}... | collective-permute-start | bytes 1572872 | tf_op jit(solution)/shard_map/ppermute | solution.py:22
  291.3 9.3 %collective-permute-done.3 = bf16[4,256,256]{2,1,0:T(8,128)(2,1)S(1)} collective-permute-done((bf16[4,256,256]{2,1,0:T(8,128)(2,1)S(1)}, bf16[4,256,256]{2,1,0:T(8,128)(2,1)S(1)}, u32[]{:S(2)}, u32[]{:S(2)}) %collective-permute-start.3) | collective-permute-done | bytes 524320 | tf_op jit(solution)/shard_map/ppermute | solution.py:20
  300.6 6.0 %collective-permute-done.2 = bf16[4,256,256]{2,1,0:T(8,128)(2,1)S(1)} collective-permute-done((bf16[4,256,256]{2,1,0:T(8,128)(2,1)S(1)}, bf16[4,256,256]{2,1,0:T(8,128)(2,1)S(1)}, u32[]{:S(2)}, u32[]{:S(2)}) %collective-permute-start.2) | collective-permute-done | bytes 524320 | tf_op jit(solution)/shard_map/ppermute | solution.py:22
  306.5 4.7 %fusion.15 = f32[8,256,256]{2,1,0:T(8,128)} fusion(bf16[8,256,256]{2,1,0:T(8,128)(2,1)S(1)} %bitcast.60, bf16[4,256,256]{2,1,0:T(8,128)(2,1)S(1)} %collective-permute-done.3, bf16[4,256,256]{2,1,0:T(8,128)(2,1)S(1)} %collective-permute-done.2, s32[256]{0:T(256)S(1)} %get-tuple-element.17, s32[256]{0:T(256)S(1)} %get-tuple-element.18), kind=kOutput, calls=%fused_computation.38 | convolution fusion | flops 1633288192 | bytes 5246976 | tf_op jit(solution)/shard_map/pq,zqb->zpb/dot_general | solution.py:54
  311.2 47.2 %all-reduce.5.cloned.1.call-done = f32[2048,256]{1,0:T(8,128)} async-done(((f32[2048,256]{1,0:T(8,128)}), f32[2048,256]{1,0:T(8,128)}) %all-reduce.5.cloned.1.call-update) | async-done | bytes 2097168 | tf_op jit(solution)/shard_map/psum | solution.py:117
  358.4 3.9 %fusion.10 = bf16[2048,256]{1,0:T(8,128)(2,1)} fusion(bf16[2048,256]{1,0:T(8,128)(2,1)S(1)} %copy-done.1, f32[2048,256]{1,0:T(8,128)} %all-reduce.5.cloned.1.call-done, bf16[2048,256]{1,0:T(8,128)(2,1)S(1)} %fusion.9, f32[8,256,256]{2,1,0:T(8,128)} %fusion.15, f32[2048]{0:T(1024)S(1)} %copy-done.2), kind=kLoop, calls=%fused_computation.32 | loop fusion | flops 5242880 | bytes 7348224 | tf_op jit(solution)/shard_map/convert_element_type | solution.py:89
  (20 shorter events, 0.5 us)
Async XLA Ops:
  6.5 84.2 %all-gather.3.cloned.1.call-start = ((), (), s32[]{:S(2)}) async-start(), calls=%async_computation | async-start | bytes 2129920 | tf_op jit(solution)/shard_map/all_gather | solution.py:106
  9.9 176.8 %all-reduce.3.cloned.1.call-start = ((), (), s32[]{:S(2)}) async-start(), calls=%async_computation.1 | async-start | bytes 4194304 | tf_op jit(solution)/shard_map/psum | solution.py:117
  23.5 75.7 %copy-start.1 = (bf16[2048,256]{1,0:T(8,128)(2,1)S(1)}, bf16[2048,256]{1,0:T(8,128)(2,1)}, u32[]{:S(2)}) copy-start(bf16[2048,256]{1,0:T(8,128)(2,1)} %param.9) | copy-start | bytes 3145732
  104.1 3.2 copy-start
  111.6 155.7 %all-gather.5.cloned.1.call-start = ((), (), s32[]{:S(2)}) async-start(), calls=%async_computation.2 | async-start | bytes 2129920 | tf_op jit(solution)/shard_map/all_gather | solution.py:106
  111.7 17.2 %collective-permute-start.1 = (bf16[4,256,256]{2,1,0:T(8,128)(2,1)S(1)}, bf16[4,256,256]{2,1,0:T(8,128)(2,1)S(1)}, u32[]{:S(2)}, u32[]{:S(2)}) collective-permute-start(bf16[4,256,256]{2,1,0:T(8,128)(2,1)S(1)} %bitcast.62), channel_id=1, source_target_pairs={{0,4},{4,8},{8,12},{12,16},{16,20},{20,24},{24,28},{28,32},{32,36}... | collective-permute-start | bytes 1572872 | tf_op jit(solution)/shard_map/ppermute | solution.py:20
  114.3 20.5 %collective-permute-start = (bf16[4,256,256]{2,1,0:T(8,128)(2,1)S(1)}, bf16[4,256,256]{2,1,0:T(8,128)(2,1)S(1)}, u32[]{:S(2)}, u32[]{:S(2)}) collective-permute-start(bf16[4,256,256]{2,1,0:T(8,128)(2,1)S(1)} %bitcast.61), channel_id=1, source_target_pairs={{4,0},{8,4},{12,8},{16,12},{20,16},{24,20},{28,24},{32,28},{36,32}... | collective-permute-start | bytes 1572872 | tf_op jit(solution)/shard_map/ppermute | solution.py:22
  134.8 52.0 %copy-start.2 = (f32[2048]{0:T(1024)S(1)}, f32[2048]{0:T(1024)}, u32[]{:S(2)}) copy-start(f32[2048]{0:T(1024)} %param.10) | copy-start | bytes 24580
  191.0 167.4 %all-reduce.5.cloned.1.call-start = ((), (), s32[]{:S(2)}) async-start(), calls=%async_computation.3 | async-start | bytes 4194304 | tf_op jit(solution)/shard_map/psum | solution.py:117
  283.4 17.2 %collective-permute-start.3 = (bf16[4,256,256]{2,1,0:T(8,128)(2,1)S(1)}, bf16[4,256,256]{2,1,0:T(8,128)(2,1)S(1)}, u32[]{:S(2)}, u32[]{:S(2)}) collective-permute-start(bf16[4,256,256]{2,1,0:T(8,128)(2,1)S(1)} %bitcast.64), channel_id=1, source_target_pairs={{0,4},{4,8},{8,12},{12,16},{16,20},{20,24},{24,28},{28,32},{32,36}... | collective-permute-start | bytes 1572872 | tf_op jit(solution)/shard_map/ppermute | solution.py:20
  285.9 20.6 %collective-permute-start.2 = (bf16[4,256,256]{2,1,0:T(8,128)(2,1)S(1)}, bf16[4,256,256]{2,1,0:T(8,128)(2,1)S(1)}, u32[]{:S(2)}, u32[]{:S(2)}) collective-permute-start(bf16[4,256,256]{2,1,0:T(8,128)(2,1)S(1)} %bitcast.63), channel_id=1, source_target_pairs={{4,0},{8,4},{12,8},{16,12},{20,16},{24,20},{28,24},{32,28},{36,32}... | collective-permute-start | bytes 1572872 | tf_op jit(solution)/shard_map/ppermute | solution.py:22
Sparse Core Ops, SparseCore 0:
  10.6 80.0 all-gather.2
  111.7 74.9 all-reduce.2
  191.1 76.1 all-gather.4
  283.4 74.9 all-reduce.4
where the time goes:
time: 369 us
  waiting for transfers between devices  267 us (72%)
  local copies, waits for them, and re-layouts  36.2 us (10%)
  matrix products  27 us (7%)
  starting transfers between devices  16.1 us (4%)
  between operations  13.2 us (4%)
  other arithmetic  9.22 us (2%)
    all_gather x2, waiting for transfers between devices, gather_points(): gathered = lax.all_gather(picked, 'slab', axis=0, tiled=True)  143 us
    psum x2, waiting for transfers between devices, apply_whole(): exch_term = lax.psum(partial_value, 'pt')  93.5 us
    ppermute x2, waiting for transfers between devices, extended(): lax.ppermute(tail, axis, [(i, (i + 1) % count) for i in range(count)])  18.6 us
    gather x2, local copies, waits for them, and re-layouts, gather_points(): return jnp.take(gathered, positions, axis=0)  17 us
    unnamed x7, local copies, waits for them, and re-layouts  15.5 us
    ppermute x2, waiting for transfers between devices, extended(): lax.ppermute(head, axis, [((i + 1) % count, i) for i in range(count)])  11.9 us
    dot_general x2, matrix products, apply_whole(): jnp.dot(kernel, field_points, preferred_element_type=jnp.float32)  11.7 us
    ppermute x2, starting transfers between devices, extended(): lax.ppermute(head, axis, [((i + 1) % count, i) for i in range(count)])  10.7 us
  transfers between devices with their start and end apart: 8, of which 8 were waited for; matrix products, arithmetic and copies ran while one was open for 7% of the time, Pallas kernels for 0%

commit v1 on v0

--- a/solution.py
+++ b/solution.py
@@ -114,7 +114,7 @@
 
     def apply_whole(vectors, field_points):
         partial_value = jnp.dot(kernel, field_points, preferred_element_type=jnp.float32)
-        exch_term = lax.psum(partial_value, "pt")
+        exch_term = jnp.sum(lax.all_gather(partial_value, "pt"), axis=0)
         return local_terms(vectors, potential) - exch_term
 
     return chebyshev(orbitals, psi_points, apply_whole, gather_points)

time: 369 us -> 423 us (1.15)
  waiting for transfers between devices: 267 us -> 316 us
  other arithmetic: 9.22 us -> 20.3 us
  starting transfers between devices: 16.1 us -> 10.3 us
    all_gather x0 -> x2, waiting for transfers between devices: none -> 139 us  [apply_whole(): exch_term = jnp.sum(lax.all_gather(partial_value, 'pt'), axis=0)]
    psum x2 -> x0, waiting for transfers between devices: 93.5 us -> none  [apply_whole(): exch_term = lax.psum(partial_value, 'pt')]
    ppermute x2, waiting for transfers between devices: 11.9 us -> 38.3 us  [extended(): lax.ppermute(head, axis, [((i + 1) % count, i) for i in range(count)])]
    ppermute x2, waiting for transfers between devices: 18.6 us -> 0.01 us  [extended(): lax.ppermute(tail, axis, [(i, (i + 1) % count) for i in range(count)])]
    reduce_sum x0 -> x2, other arithmetic: none -> 11.1 us  [apply_whole(): exch_term = jnp.sum(lax.all_gather(partial_value, 'pt'), axis=0)]
    ppermute x2, starting transfers between devices: 5.08 us -> 0.01 us  [extended(): lax.ppermute(tail, axis, [(i, (i + 1) % count) for i in range(count)])]
    all_gather x2, waiting for transfers between devices: 143 us -> 139 us  [gather_points(): gathered = lax.all_gather(picked, 'slab', axis=0, tiled=True)]
  transfers between devices with their start and end apart: 8 -> 8, of which waited for: 8 -> 6; matrix products, arithmetic and copies ran while one was open for 7% -> 6% of each run, Pallas kernels for 0% -> 0%
where the time goes in v1:
time: 423 us
  waiting for transfers between devices  316 us (75%)
  local copies, waits for them, and re-layouts  36.2 us (9%)
  matrix products  26.9 us (6%)
  other arithmetic  20.3 us (5%)
  between operations  13.2 us (3%)
  starting transfers between devices  10.3 us (2%)
    all_gather x2, waiting for transfers between devices, gather_points(): gathered = lax.all_gather(picked, 'slab', axis=0, tiled=True)  139 us
    all_gather x2, waiting for transfers between devices, apply_whole(): exch_term = jnp.sum(lax.all_gather(partial_value, 'pt'), axis=0)  139 us
    ppermute x2, waiting for transfers between devices, extended(): lax.ppermute(head, axis, [((i + 1) % count, i) for i in range(count)])  38.3 us
    gather x2, local copies, waits for them, and re-layouts, gather_points(): return jnp.take(gathered, positions, axis=0)  17 us
    unnamed x7, local copies, waits for them, and re-layouts  15.5 us
    dot_general x2, matrix products, apply_whole(): jnp.dot(kernel, field_points, preferred_element_type=jnp.float32)  11.7 us
    reduce_sum x2, other arithmetic, apply_whole(): exch_term = jnp.sum(lax.all_gather(partial_value, 'pt'), axis=0)  11.1 us
    dot_general x2, matrix products, local_terms(): jnp.einsum('pq,zqb->zpb', plane_table(), center, precision=lax.Precision....  10.4 us
  transfers between devices with their start and end apart: 8, of which 6 were waited for; matrix products, arithmetic and copies ran while one was open for 6% of the time, Pallas kernels for 0%

profile of v1, /device:TPU:1, one launch (start us, length us, event | category | flops | bytes accessed | tf_op | source)
XLA Modules:
  0.0 422.8 jit_solution(12359619489950337764)
XLA Ops:
  6.5 0.7 compare_and_fusion.16
  7.2 2.0 gather_fusion
  9.2 0.7 broadcast_select_fusion.4
  10.0 0.7 fusion.52
  10.7 0.1 copy.11
  10.8 0.1 reduce-window.8
  10.9 0.1 reduce
  11.0 12.3 %copy.10 = bf16[2048,2048]{0,1:T(8,128)(2,1)} copy(bf16[2048,2048]{1,0:T(8,128)(2,1)} %param.11) | data formatting | bytes 16777216 | tf_op args[2]
  23.3 0.2 convert_reduce_fusion
  23.5 67.2 %all-gather.7.cloned.1.call-done = bf16[4096,256]{1,0:T(8,128)(2,1)} async-done(((bf16[64,256]{1,0:T(8,128)(2,1)}), bf16[4096,256]{1,0:T(8,128)(2,1)}) %all-gather.7.cloned.1.call-update) | async-done | bytes 2097168 | tf_op jit(solution)/shard_map/all_gather | solution.py:106
  90.7 8.5 %gather_fusion.1 = bf16[2048,256]{1,0:T(8,128)(2,1)S(1)} fusion(bf16[4096,256]{1,0:T(8,128)(2,1)} %all-gather.7.cloned.1.call-done, s32[2048]{0:T(1024)S(1)} %broadcast_clamp_fusion), kind=kCustom, calls=%fused_computation.1.clone | custom fusion | bytes 2105344 | tf_op jit(solution)/shard_map/jit(_take)/gather | solution.py:107
  99.3 4.8 %fusion = bf16[2048,2048]{0,1:T(8,128)(2,1)S(1)} fusion(bf16[2048,2048]{0,1:T(8,128)(2,1)} %copy.10, bf16[2048,256]{1,0:T(8,128)(2,1)S(1)} %copy-done.1, bf16[2048,256]{1,0:T(8,128)(2,1)S(1)} %gather_fusion.1, pred[2048]{0:T(1024)(128)(4,1)S(1)} %compare_and_fusion.15), kind=kOutput, calls=%fused_computation.5 | convolution fusion | flops 2160590848 | bytes 18876416 | tf_op jit(solution)/shard_map/dot_general | solution.py:110
  104.1 3.2 copy-done
  107.3 4.2 fusion.37
  111.7 5.0 %collective-permute-start = (bf16[4,256,256]{2,1,0:T(8,128)(2,1)S(1)}, bf16[4,256,256]{2,1,0:T(8,128)(2,1)S(1)}, u32[]{:S(2)}, u32[]{:S(2)}) collective-permute-start(bf16[4,256,256]{2,1,0:T(8,128)(2,1)S(1)} %bitcast.66), channel_id=1, source_target_pairs={{4,0},{8,4},{12,8},{16,12},{20,16},{24,20},{28,24},{32,28},{36,32}... | collective-permute-start | bytes 1572872 | tf_op jit(solution)/shard_map/ppermute | solution.py:22
  116.7 19.1 %collective-permute-done = bf16[4,256,256]{2,1,0:T(8,128)(2,1)S(1)} collective-permute-done((bf16[4,256,256]{2,1,0:T(8,128)(2,1)S(1)}, bf16[4,256,256]{2,1,0:T(8,128)(2,1)S(1)}, u32[]{:S(2)}, u32[]{:S(2)}) %collective-permute-start) | collective-permute-done | bytes 524320 | tf_op jit(solution)/shard_map/ppermute | solution.py:22
  135.8 5.7 %fusion.20 = f32[8,256,256]{2,1,0:T(8,128)} fusion(bf16[8,256,256]{2,1,0:T(8,128)(2,1)S(1)} %bitcast.61, bf16[4,256,256]{2,1,0:T(8,128)(2,1)S(1)} %collective-permute-done.1, bf16[4,256,256]{2,1,0:T(8,128)(2,1)S(1)} %collective-permute-done, s32[256]{0:T(256)S(1)} %get-tuple-element.17, s32[256]{0:T(256)S(1)} %get-tuple-element.18), kind=kOutput, calls=%fused_computation.44 | convolution fusion | flops 1633288192 | bytes 5246976 | tf_op jit(solution)/shard_map/pq,zqb->zpb/dot_general | solution.py:54
  141.5 68.9 %all-gather.11.cloned.1.call-done = f32[8192,256]{1,0:T(8,128)} async-done(((f32[2048,256]{1,0:T(8,128)}), f32[8192,256]{1,0:T(8,128)}) %all-gather.11.cloned.1.call-update) | async-done | bytes 8388624 | tf_op jit(solution)/shard_map/all_gather | solution.py:117
  210.3 5.5 %reduce_sum.38 = f32[2048,256]{1,0:T(8,128)} reduce(f32[4,2048,256]{2,1,0:T(8,128)} %bitcast.63, f32[]{:T(128)} %constant.143.clone.1), dimensions={0}, to_apply=%region_3.6 | reduce | flops 1572864 | bytes 10485764 | tf_op jit(solution)/shard_map/reduce_sum | solution.py:117
  215.9 2.8 fusion.9
  218.7 0.7 gather_fusion.2
  219.4 0.7 broadcast_select_fusion.3
  220.1 0.2 all-gather.13.cloned.1.call-start
  220.3 71.7 %all-gather.9.cloned.1.call-done = bf16[4096,256]{1,0:T(8,128)(2,1)} async-done(((bf16[64,256]{1,0:T(8,128)(2,1)}), bf16[4096,256]{1,0:T(8,128)(2,1)}) %all-gather.9.cloned.1.call-update) | async-done | bytes 2097168 | tf_op jit(solution)/shard_map/all_gather | solution.py:106
  292.0 8.5 %gather_fusion.3 = bf16[2048,256]{1,0:T(8,128)(2,1)S(1)} fusion(bf16[4096,256]{1,0:T(8,128)(2,1)} %all-gather.9.cloned.1.call-done, s32[2048]{0:T(1024)S(1)} %broadcast_clamp_fusion), kind=kCustom, calls=%fused_computation.3.clone | custom fusion | bytes 2105344 | tf_op jit(solution)/shard_map/jit(_take)/gather | solution.py:107
  300.5 7.5 %fusion.33 = f32[2048,256]{1,0:T(8,128)} fusion(bf16[2048,2048]{0,1:T(8,128)(2,1)} %copy-done, bf16[2048,256]{1,0:T(8,128)(2,1)S(1)} %gather_fusion.3, pred[2048]{0:T(1024)(128)(4,1)S(1)} %compare_and_fusion.15), kind=kOutput, calls=%fused_computation.73 | convolution fusion | flops 2148007936 | bytes 11536384 | tf_op jit(solution)/shard_map/dot_general | solution.py:116
  308.1 5.0 %collective-permute-start.2 = (bf16[4,256,256]{2,1,0:T(8,128)(2,1)S(1)}, bf16[4,256,256]{2,1,0:T(8,128)(2,1)S(1)}, u32[]{:S(2)}, u32[]{:S(2)}) collective-permute-start(bf16[4,256,256]{2,1,0:T(8,128)(2,1)S(1)} %bitcast.68), channel_id=1, source_target_pairs={{4,0},{8,4},{12,8},{16,12},{20,16},{24,20},{28,24},{32,28},{36,32}... | collective-permute-start | bytes 1572872 | tf_op jit(solution)/shard_map/ppermute | solution.py:22
  313.1 19.1 %collective-permute-done.2 = bf16[4,256,256]{2,1,0:T(8,128)(2,1)S(1)} collective-permute-done((bf16[4,256,256]{2,1,0:T(8,128)(2,1)S(1)}, bf16[4,256,256]{2,1,0:T(8,128)(2,1)S(1)}, u32[]{:S(2)}, u32[]{:S(2)}) %collective-permute-start.2) | collective-permute-done | bytes 524320 | tf_op jit(solution)/shard_map/ppermute | solution.py:22
  332.2 4.7 %fusion.15 = f32[8,256,256]{2,1,0:T(8,128)} fusion(bf16[8,256,256]{2,1,0:T(8,128)(2,1)S(1)} %bitcast.62, bf16[4,256,256]{2,1,0:T(8,128)(2,1)S(1)} %collective-permute-done.3, bf16[4,256,256]{2,1,0:T(8,128)(2,1)S(1)} %collective-permute-done.2, s32[256]{0:T(256)S(1)} %get-tuple-element.17, s32[256]{0:T(256)S(1)} %get-tuple-element.18), kind=kOutput, calls=%fused_computation.38 | convolution fusion | flops 1633288192 | bytes 5246976 | tf_op jit(solution)/shard_map/pq,zqb->zpb/dot_general | solution.py:54
  337.0 69.8 %all-gather.13.cloned.1.call-done = f32[8192,256]{1,0:T(8,128)} async-done(((f32[2048,256]{1,0:T(8,128)}), f32[8192,256]{1,0:T(8,128)}) %all-gather.13.cloned.1.call-update) | async-done | bytes 8388624 | tf_op jit(solution)/shard_map/all_gather | solution.py:117
  406.7 5.6 %reduce_sum.39 = f32[2048,256]{1,0:T(8,128)} reduce(f32[4,2048,256]{2,1,0:T(8,128)} %bitcast.64, f32[]{:T(128)} %constant.143.clone.1), dimensions={0}, to_apply=%region_4.7 | reduce | flops 1572864 | bytes 10485764 | tf_op jit(solution)/shard_map/reduce_sum | solution.py:117
  412.3 3.9 fusion.10
  (22 shorter events, 0.3 us)
Async XLA Ops:
  6.5 84.2 %all-gather.7.cloned.1.call-start = ((), (), s32[]{:S(2)}) async-start(), calls=%async_computation | async-start | bytes 2129920 | tf_op jit(solution)/shard_map/all_gather | solution.py:106
  9.9 200.4 %all-gather.11.cloned.1.call-start = ((), (), s32[]{:S(2)}) async-start(), calls=%async_computation.2 | async-start | bytes 10485760 | tf_op jit(solution)/shard_map/all_gather | solution.py:117
  23.5 75.7 %copy-start.1 = (bf16[2048,256]{1,0:T(8,128)(2,1)S(1)}, bf16[2048,256]{1,0:T(8,128)(2,1)}, u32[]{:S(2)}) copy-start(bf16[2048,256]{1,0:T(8,128)(2,1)} %param.9) | copy-start | bytes 3145732
  104.1 3.2 copy-start
  111.6 180.4 %all-gather.9.cloned.1.call-start = ((), (), s32[]{:S(2)}) async-start(), calls=%async_computation.1 | async-start | bytes 2129920 | tf_op jit(solution)/shard_map/all_gather | solution.py:106
  111.7 24.1 %collective-permute-start = (bf16[4,256,256]{2,1,0:T(8,128)(2,1)S(1)}, bf16[4,256,256]{2,1,0:T(8,128)(2,1)S(1)}, u32[]{:S(2)}, u32[]{:S(2)}) collective-permute-start(bf16[4,256,256]{2,1,0:T(8,128)(2,1)S(1)} %bitcast.66), channel_id=1, source_target_pairs={{4,0},{8,4},{12,8},{16,12},{20,16},{24,20},{28,24},{32,28},{36,32}... | collective-permute-start | bytes 1572872 | tf_op jit(solution)/shard_map/ppermute | solution.py:22
  116.7 19.1 %collective-permute-start.1 = (bf16[4,256,256]{2,1,0:T(8,128)(2,1)S(1)}, bf16[4,256,256]{2,1,0:T(8,128)(2,1)S(1)}, u32[]{:S(2)}, u32[]{:S(2)}) collective-permute-start(bf16[4,256,256]{2,1,0:T(8,128)(2,1)S(1)} %bitcast.65), channel_id=1, source_target_pairs={{0,4},{4,8},{8,12},{12,16},{16,20},{20,24},{24,28},{28,32},{32,36}... | collective-permute-start | bytes 1572872 | tf_op jit(solution)/shard_map/ppermute | solution.py:20
  210.3 5.5 %copy-start.2 = (f32[2048]{0:T(1024)S(1)}, f32[2048]{0:T(1024)}, u32[]{:S(2)}) copy-start(f32[2048]{0:T(1024)} %param.10) | copy-start | bytes 24580
  220.1 186.6 %all-gather.13.cloned.1.call-start = ((), (), s32[]{:S(2)}) async-start(), calls=%async_computation.3 | async-start | bytes 10485760 | tf_op jit(solution)/shard_map/all_gather | solution.py:117
  308.1 24.1 %collective-permute-start.2 = (bf16[4,256,256]{2,1,0:T(8,128)(2,1)S(1)}, bf16[4,256,256]{2,1,0:T(8,128)(2,1)S(1)}, u32[]{:S(2)}, u32[]{:S(2)}) collective-permute-start(bf16[4,256,256]{2,1,0:T(8,128)(2,1)S(1)} %bitcast.68), channel_id=1, source_target_pairs={{4,0},{8,4},{12,8},{16,12},{20,16},{24,20},{28,24},{32,28},{36,32}... | collective-permute-start | bytes 1572872 | tf_op jit(solution)/shard_map/ppermute | solution.py:22
  313.1 19.1 %collective-permute-start.3 = (bf16[4,256,256]{2,1,0:T(8,128)(2,1)S(1)}, bf16[4,256,256]{2,1,0:T(8,128)(2,1)S(1)}, u32[]{:S(2)}, u32[]{:S(2)}) collective-permute-start(bf16[4,256,256]{2,1,0:T(8,128)(2,1)S(1)} %bitcast.67), channel_id=1, source_target_pairs={{0,4},{4,8},{8,12},{12,16},{16,20},{20,24},{24,28},{28,32},{32,36}... | collective-permute-start | bytes 1572872 | tf_op jit(solution)/shard_map/ppermute | solution.py:20
Sparse Core Ops, SparseCore 0:
  10.6 80.0 all-gather.6
  111.7 98.6 all-gather.10
  220.2 71.7 all-gather.8
  308.1 98.5 all-gather.12
